TPU v7x, 32 devices: a whole 2x2x4 slice. The times are simulated.
32 devices in a mesh: section: 2 (over core), seq: 4 (over y, x), tensor: 4 (over z).
Axes of the slice: x: 2, y: 2, z: 4, core: 2. Of those that a mesh axis runs over, the one named last changes fastest.
Arguments:
- tokens: bfloat16 [4096, 1024], P('seq', 'tensor'), may hold values from -6 to 6
- segments: int32 [8, 512], P('seq'), may hold values from 0 to 3, never falling along the last dimension, each value on 1 to 256 neighbouring positions
- cotangent: bfloat16 [4096, 1024], P('seq', 'tensor'), may hold values from -6 to 6
- norm1_gain: bfloat16 [2, 1024], P('section', ('tensor', 'seq')), may hold values from 0.5 to 1.5
- norm1_bias: bfloat16 [2, 1024], P('section', ('tensor', 'seq')), may hold values from -3 to 3
- qkv_weight: bfloat16 [2, 1024, 16, 192], P('section', 'seq', 'tensor'), may hold values from -0.1875 to 0.1875
- qv_bias: bfloat16 [2, 16, 128], P('section', 'tensor', 'seq'), may hold values from -4 to 4
- out_weight: bfloat16 [2, 16, 64, 1024], P('section', 'tensor', None, 'seq'), may hold values from -0.75 to 0.75
- out_bias: bfloat16 [2, 1024], P('section', ('tensor', 'seq')), may hold values from -3 to 3
- norm2_gain: bfloat16 [2, 1024], P('section', ('tensor', 'seq')), may hold values from 0.5 to 1.5
- norm2_bias: bfloat16 [2, 1024], P('section', ('tensor', 'seq')), may hold values from -3 to 3
- up_weight: bfloat16 [2, 1024, 4096], P('section', 'seq', 'tensor'), may hold values from -0.1875 to 0.1875
- up_bias: bfloat16 [2, 4096], P('section', ('tensor', 'seq')), may hold values from -4 to 4
- down_weight: bfloat16 [2, 4096, 1024], P('section', 'tensor', 'seq'), may hold values from -0.09375 to 0.09375
- down_bias: bfloat16 [2, 1024], P('section', ('tensor', 'seq')), may hold values from -3 to 3
Outputs:
- section_out: bfloat16 [2, 4096, 1024], P('section', 'seq', 'tensor')
- input_grad: bfloat16 [2, 4096, 1024], P('section', 'seq', 'tensor')
- grad_norm1_gain: float32 [2, 1024], P('section', ('tensor', 'seq'))
- grad_norm1_bias: float32 [2, 1024], P('section', ('tensor', 'seq'))
- grad_qkv_weight: float32 [2, 1024, 16, 192], P('section', 'seq', 'tensor')
- grad_qv_bias: float32 [2, 16, 128], P('section', 'tensor', 'seq')
- grad_out_weight: float32 [2, 16, 64, 1024], P('section', 'tensor', None, 'seq')
- grad_out_bias: float32 [2, 1024], P('section', ('tensor', 'seq'))
- grad_norm2_gain: float32 [2, 1024], P('section', ('tensor', 'seq'))
- grad_norm2_bias: float32 [2, 1024], P('section', ('tensor', 'seq'))
- grad_up_weight: float32 [2, 1024, 4096], P('section', 'seq', 'tensor')
- grad_up_bias: float32 [2, 4096], P('section', ('tensor', 'seq'))
- grad_down_weight: float32 [2, 4096, 1024], P('section', 'tensor', 'seq')
- grad_down_bias: float32 [2, 1024], P('section', ('tensor', 'seq'))
Inputs may be any that keep to these rules, and one draw needn't show every extreme that they name: `segments`: along each sequence the document numbers never fall; every document holds 1 to 256 positions.
All inputs are finite; a program needn't handle non-finite values.
Results may differ from a plain program's by a relative error of at most 0.02.
Values may be sent and summed in bfloat16 or wider, within the bound.
A program may use at most 192 MiB of HBM per device.

v0:
```python
import functools
import math
import jax
import jax.numpy as jnp
from jax import lax
from jax.sharding import PartitionSpec as P

epsilon = 1e-05
floor_value = -1e30
f32 = jnp.float32
bf16 = jnp.bfloat16


def gather_columns(piece):
    return lax.all_gather(piece, "tensor", axis=1, tiled=True)


def gather_rows(piece):
    return lax.all_gather(piece, "tensor", axis=0, tiled=True)


def scatter_rows(partial_rows):
    return lax.psum_scatter(
        partial_rows.astype(bf16), "tensor", scatter_dimension=0, tiled=True
    ).astype(f32)


def norm_parts(rows):
    average = jnp.mean(rows, axis=1, keepdims=True)
    variance = jnp.mean(rows * rows, axis=1, keepdims=True) - average * average
    scale = lax.rsqrt(variance + epsilon)
    return ((rows - average) * scale, scale)


def norm_backward(grad, centred, scale, gain):
    scaled = grad * gain
    total = jnp.mean(scaled, axis=1, keepdims=True)
    along = jnp.mean(scaled * centred, axis=1, keepdims=True)
    return scale * (scaled - total - centred * along)


def allowed_mask(segment):
    length = segment.shape[1]
    place = lax.broadcasted_iota(jnp.int32, (length, length), 0)
    other = lax.broadcasted_iota(jnp.int32, (length, length), 1)
    same = segment[:, :, None] == segment[:, None, :]
    return (same & (other <= place)[None])[:, None]


def gelu_value(upper):
    return jax.nn.gelu(upper, approximate=True)


def dot(left, right, dims):
    return lax.dot_general(left, right, (dims, ((), ())), preferred_element_type=f32)


def forward(whole, rows, mask, weights):
    gain1, bias1, w_qkv, b_qv, w_out, b_out, gain2, bias2, w_up, b_up, w_down, b_down = weights
    count = whole.shape[0]
    heads, wide = w_qkv.shape[1:]
    size = wide // 3
    shape4 = (mask.shape[0], mask.shape[2], heads, size)
    factor = 1.0 / math.sqrt(size)
    normed = (norm_parts(whole.astype(f32))[0] * gain1 + bias1).astype(bf16)
    rows = rows.astype(f32)
    centred1, scale1 = norm_parts(rows)
    mixed = jnp.einsum("rd,dhe->rhe", normed, w_qkv, preferred_element_type=f32)
    query = (mixed[..., :size] + b_qv[:, :size]).astype(bf16).reshape(shape4)
    keys = mixed[..., size : 2 * size].astype(bf16).reshape(shape4)
    values = (mixed[..., 2 * size :] + b_qv[:, size:]).astype(bf16).reshape(shape4)
    scores = jnp.einsum("sqhe,skhe->shqk", query, keys, preferred_element_type=f32) * factor
    masked = jnp.where(mask, scores, floor_value)
    raised = jnp.exp(masked - jnp.max(masked, axis=-1, keepdims=True))
    chance = raised / jnp.sum(raised, axis=-1, keepdims=True)
    low = chance.astype(bf16)
    context = jnp.einsum("shqk,skhe->sqhe", low, values, preferred_element_type=f32)
    context = context.reshape(count, heads * size).astype(bf16)
    attn = scatter_rows(dot(context, w_out, ((1,), (0,)))) + b_out
    hidden = rows + attn
    centred2, scale2 = norm_parts(hidden)
    normed2 = gather_rows((centred2 * gain2 + bias2).astype(bf16))
    upper = dot(normed2, w_up, ((1,), (0,))) + b_up
    active = gelu_value(upper).astype(bf16)
    branch = scatter_rows(dot(active, w_down, ((1,), (0,)))) + b_down
    output = (hidden + branch).astype(bf16)
    kept = (
        centred1,
        scale1,
        normed,
        query,
        keys,
        values,
        chance,
        low,
        context,
        centred2,
        scale2,
        normed2,
        upper,
        active,
    )
    return (output, kept)


def backward(grad_whole, grad_rows, weights, kept):
    gain1, bias1, w_qkv, b_qv, w_out, b_out, gain2, bias2, w_up, b_up, w_down, b_down = weights
    (
        centred1,
        scale1,
        normed,
        query,
        keys,
        values,
        chance,
        low,
        context,
        centred2,
        scale2,
        normed2,
        upper,
        active,
    ) = kept
    count = grad_whole.shape[0]
    heads, wide = w_qkv.shape[1:]
    size = wide // 3
    factor = 1.0 / math.sqrt(size)
    grad_out = grad_rows.astype(f32)
    grad_active = dot(grad_whole, w_down, ((1,), (1,)))
    grad_upper = jax.vjp(gelu_value, upper)[1](grad_active)[0].astype(bf16)
    grad_normed2 = scatter_rows(dot(grad_upper, w_up, ((1,), (1,))))
    grad_down = dot(active, grad_whole, ((0,), (0,)))
    grad_up = dot(normed2, grad_upper, ((0,), (0,)))
    grad_hidden = grad_out + norm_backward(grad_normed2, centred2, scale2, gain2)
    grad_attn = grad_hidden.astype(bf16)
    attn_whole = gather_rows(grad_attn)
    grad_context = dot(attn_whole, w_out, ((1,), (1,))).astype(bf16).reshape(query.shape)
    grad_out_w = dot(context, attn_whole, ((0,), (0,)))
    grad_chance = jnp.einsum("sqhe,skhe->shqk", grad_context, values, preferred_element_type=f32)
    delta = jnp.sum(grad_chance * chance, axis=-1, keepdims=True)
    grad_scores = (chance * (grad_chance - delta)).astype(bf16)
    grad_query = (
        jnp.einsum("shqk,skhe->sqhe", grad_scores, keys, preferred_element_type=f32) * factor
    ).astype(bf16)
    grad_keys = (
        jnp.einsum("shqk,sqhe->skhe", grad_scores, query, preferred_element_type=f32) * factor
    ).astype(bf16)
    grad_values = jnp.einsum(
        "shqk,sqhe->skhe", low, grad_context, preferred_element_type=f32
    ).astype(bf16)
    grad_mixed = jnp.concatenate([grad_query, grad_keys, grad_values], axis=-1).reshape(
        count, heads, wide
    )
    grad_normed1 = scatter_rows(
        jnp.einsum("rhe,dhe->rd", grad_mixed, w_qkv, preferred_element_type=f32)
    )
    grad_qkv = jnp.einsum("rd,rhe->dhe", normed, grad_mixed, preferred_element_type=f32)
    grad_qv = jnp.concatenate(
        [
            jnp.sum(grad_query.astype(f32), axis=(0, 1)),
            jnp.sum(grad_values.astype(f32), axis=(0, 1)),
        ],
        axis=-1,
    )
    grad_input = grad_hidden + norm_backward(grad_normed1, centred1, scale1, gain1)
    vectors = (
        jnp.sum(grad_normed1 * centred1, axis=0),
        jnp.sum(grad_normed1, axis=0),
        jnp.sum(grad_attn.astype(f32), axis=0),
        jnp.sum(grad_normed2 * centred2, axis=0),
        jnp.sum(grad_normed2, axis=0),
        jnp.sum(grad_out, axis=0),
    )
    local = (jnp.sum(grad_upper.astype(f32), axis=0), grad_qv)
    return (grad_input.astype(bf16), (grad_qkv, grad_out_w, grad_up, grad_down), vectors, local)


def swap(item):
    return lax.ppermute(item, "section", [(0, 1), (1, 0)])


def body(
    tokens,
    segments,
    cotangent,
    norm1_gain,
    norm1_bias,
    qkv_weight,
    qv_bias,
    out_weight,
    out_bias,
    norm2_gain,
    norm2_bias,
    up_weight,
    up_bias,
    down_weight,
    down_bias,
):
    section = lax.axis_index("section")
    place = lax.axis_index("tensor")
    tensors = lax.axis_size("tensor")
    quads = lax.axis_size("seq")
    first = section == 0
    rows_all, width = tokens.shape
    count = rows_all // 2
    block = count // tensors
    full = width * tensors
    heads, wide = qkv_weight.shape[2:]
    size = wide // 3
    part = norm1_gain.shape[1]
    part_up = up_bias.shape[1]
    part_qv = qv_bias.shape[2]

    def mine(item):
        return lax.dynamic_slice_in_dim(item, section * (item.shape[0] // 2), item.shape[0] // 2, 0)

    def block_of(whole):
        return lax.dynamic_slice_in_dim(whole, place * block, block, 0)

    def columns_of(whole):
        return lax.dynamic_slice_in_dim(whole, place * width, width, 1)

    whole0 = gather_columns(mine(tokens))
    packed = jnp.concatenate(
        [
            norm1_gain[0],
            norm1_bias[0],
            out_bias[0],
            norm2_gain[0],
            norm2_bias[0],
            down_bias[0],
            up_bias[0],
            qv_bias[0].reshape(-1),
        ]
    )
    small = lax.all_gather(packed, ("section", "tensor", "seq"), axis=0, tiled=False)
    small = small.reshape(2, tensors, quads, packed.shape[0]).astype(f32)

    def pair(weight, axis):
        gathered = lax.all_gather(weight, "seq", axis=axis, tiled=True)
        return lax.all_gather(gathered, "section", axis=0, tiled=False)

    w_qkv = pair(qkv_weight[0], 0)
    w_out = pair(out_weight[0].reshape(heads * size, -1), 1)
    w_up = pair(up_weight[0], 0)
    w_down = pair(down_weight[0], 1)
    whole_cot = gather_columns(mine(cotangent))

    def weights_of(layer):
        own = small[layer]
        vectors = [own[:, :, i * part : (i + 1) * part].reshape(full) for i in range(6)]
        local = lax.dynamic_slice_in_dim(own, place, 1, 0)[0]
        b_up = local[:, 6 * part : 6 * part + part_up].reshape(-1)
        b_qv = local[:, 6 * part + part_up :].reshape(quads, heads, part_qv)
        b_qv = jnp.transpose(b_qv, (1, 0, 2)).reshape(heads, 2 * size)
        return (
            vectors[0],
            vectors[1],
            w_qkv[layer],
            b_qv,
            w_out[layer],
            vectors[2],
            vectors[3],
            vectors[4],
            w_up[layer],
            b_up,
            w_down[layer],
            vectors[5],
        )

    params = (weights_of(0), weights_of(1))
    mask = allowed_mask(mine(segments))
    out0, kept0 = forward(whole0, block_of(whole0), mask, params[0])
    whole1 = gather_rows(out0)
    out1, kept1 = forward(whole1, out0, mask, params[1])
    grad1, big1, vec1, loc1 = backward(whole_cot, block_of(whole_cot), params[1], kept1)

    def reduce_big(big):
        axes = (0, 1, 0, 1)
        return tuple(
            (
                lax.psum_scatter(item.astype(bf16), "seq", scatter_dimension=axis, tiled=True)
                for item, axis in zip(big, axes)
            )
        )

    red1 = reduce_big(big1)
    whole_grad = gather_rows(grad1)
    grad0, big0, vec0, loc0 = backward(whole_grad, grad1, params[0], kept0)
    red0 = reduce_big(big0)

    def to_columns(rows):
        return lax.all_to_all(rows, "tensor", split_axis=1, concat_axis=0, tiled=True)

    def settle(of0, of1):
        own = jnp.where(first, of0, of1)
        other = swap(jnp.where(first, of1, of0))
        return jnp.where(first, jnp.concatenate([own, other]), jnp.concatenate([other, own]))

    outputs = settle(columns_of(whole1), to_columns(out1))
    input_grads = settle(to_columns(grad0), columns_of(whole_grad))
    totals = tuple(
        (
            jnp.where(first, a, b).astype(f32) + swap(jnp.where(first, b, a)).astype(f32)
            for a, b in zip(red0, red1)
        )
    )

    def pack(vectors, local):
        rows = [item.reshape(tensors, quads, part) for item in vectors]
        up = local[0].reshape(1, quads, part_up)
        qv = jnp.transpose(local[1].reshape(heads, quads, part_qv), (1, 0, 2))
        here = jnp.concatenate([up, qv.reshape(1, quads, heads * part_qv)], axis=-1)
        ours = lax.broadcasted_iota(jnp.int32, (tensors, 1, 1), 0) == place
        rows.append(jnp.where(ours, here, 0.0))
        return jnp.concatenate(rows, axis=-1)

    vectors = jnp.stack([pack(vec0, loc0), pack(vec1, loc1)])
    vectors = vectors.reshape(2 * tensors * quads, -1)
    vectors = lax.psum_scatter(
        vectors, ("section", "tensor", "seq"), scatter_dimension=0, tiled=True
    )[0]
    small_grads = [vectors[i * part : (i + 1) * part] for i in range(6)]
    g_up = vectors[6 * part : 6 * part + part_up]
    g_qv = vectors[6 * part + part_up :].reshape(heads, part_qv)
    result = (
        outputs,
        input_grads,
        small_grads[0],
        small_grads[1],
        totals[0],
        g_qv,
        totals[1].reshape(heads, size, -1),
        small_grads[2],
        small_grads[3],
        small_grads[4],
        totals[2],
        g_up,
        totals[3],
        small_grads[5],
    )
    return tuple((item[None] for item in result))


def solution(mesh):
    return jax.shard_map(
        body,
        mesh=mesh,
        in_specs=(
            P("seq", "tensor"),
            P("seq", None),
            P("seq", "tensor"),
            P("section", ("tensor", "seq")),
            P("section", ("tensor", "seq")),
            P("section", "seq", "tensor", None),
            P("section", "tensor", "seq"),
            P("section", "tensor", None, "seq"),
            P("section", ("tensor", "seq")),
            P("section", ("tensor", "seq")),
            P("section", ("tensor", "seq")),
            P("section", "seq", "tensor"),
            P("section", ("tensor", "seq")),
            P("section", "tensor", "seq"),
            P("section", ("tensor", "seq")),
        ),
        out_specs=(
            P("section", "seq", "tensor"),
            P("section", "seq", "tensor"),
            P("section", ("tensor", "seq")),
            P("section", ("tensor", "seq")),
            P("section", "seq", "tensor", None),
            P("section", "tensor", "seq"),
            P("section", "tensor", None, "seq"),
            P("section", ("tensor", "seq")),
            P("section", ("tensor", "seq")),
            P("section", ("tensor", "seq")),
            P("section", "seq", "tensor"),
            P("section", ("tensor", "seq")),
            P("section", "tensor", "seq"),
            P("section", ("tensor", "seq")),
        ),
        check_vma=False,
    )
```

profile of v0, /device:TPU:8, one launch (start us, length us, event | category | flops | bytes accessed | tf_op | source)
XLA Modules:
  0.0 1104.5 jit_solution(2725057039113949337)
XLA Ops:
  9.0 32.7 %all-gather.41.cloned.1.call-done = bf16[1,1024,4,192]{1,3,2,0:T(8,128)(2,1)} async-done(((bf16[1,256,4,192]{1,3,2,0:T(8,128)(2,1)}), bf16[1,1024,4,192]{1,3,2,0:T(8,128)(2,1)}) %all-gather.41.cloned.1.call-update) | async-done | bytes 1572880 | tf_op jit(solution)/shard_map/all_gather | solution.py:240
  41.8 13.8 %all_gather.72 = bf16[256,1024]{1,0:T(8,128)(2,1)} all-gather(bf16[256,256]{1,0:T(8,128)(2,1)S(1)} %bitcast.220), channel_id=1, replica_groups=mesh['section'=2,'seq'=4,'tensor'=4] {'seq'}, dimensions={1}, use_global_device_ids=true | all-gather | bytes 655360 | tf_op jit(solution)/shard_map/all_gather | solution.py:240
  56.5 62.1 %all-gather.8 = bf16[32,1,768]{2,1,0:T(2,128)(2,1)S(1)} all-gather(bf16[1,1,768]{2,1,0:T(2,128)(2,1)S(1)} %reshape.655), channel_id=2, replica_groups=mesh['section'=2,'seq'=4,'tensor'=4] {'section','tensor','seq'}, dimensions={0}, use_global_device_ids=true | all-gather | bytes 50688 | tf_op jit(solution)/shard_map/all_gather | solution.py:236
  121.6 2.7 fusion.138
  124.2 2.5 fusion.135
  126.7 4.8 fusion.145
  131.5 2.9 convolution_convert_fusion.13
  134.5 2.5 convolution_convert_fusion.5
  138.8 25.6 %reduce-scatter.17.cloned.1.call-done = bf16[128,1024]{1,0:T(8,128)(2,1)} async-done(((bf16[512,1024]{1,0:T(8,128)(2,1)}), bf16[128,1024]{1,0:T(8,128)(2,1)}) %reduce-scatter.17.cloned.1.call-update) | async-done | bytes 262160 | tf_op jit(solution)/shard_map/reduce_scatter | solution.py:23
  167.5 34.4 %all-gather.51.cloned.1.call-done = bf16[1,1024,1024]{2,1,0:T(8,128)(2,1)} async-done(((bf16[1,1024,256]{2,1,0:T(8,128)(2,1)}), bf16[1,1024,1024]{2,1,0:T(8,128)(2,1)}) %all-gather.51.cloned.1.call-update) | async-done | bytes 2097168 | tf_op jit(solution)/shard_map/all_gather | solution.py:240
  202.0 15.4 %all-gather.49.cloned.1.call-done = bf16[2,1024,1024]{2,1,0:T(8,128)(2,1)} async-done(((bf16[1,1024,1024]{2,1,0:T(8,128)(2,1)}), bf16[2,1024,1024]{2,1,0:T(8,128)(2,1)}) %all-gather.49.cloned.1.call-update) | async-done | bytes 4194320 | tf_op jit(solution)/shard_map/all_gather | solution.py:241
  217.4 31.0 %all-gather.27.cloned.1.call-done = bf16[512,1024]{1,0:T(8,128)(2,1)} async-done(((bf16[128,1024]{1,0:T(8,128)(2,1)}), bf16[512,1024]{1,0:T(8,128)(2,1)}) %all-gather.27.cloned.1.call-update) | async-done | bytes 1048592 | tf_op jit(solution)/shard_map/all_gather | solution.py:19
  248.4 4.5 fusion.35
  253.0 10.3 all-gather.53.cloned.1.call-done
  263.2 4.8 fusion.46
  268.1 26.2 %reduce-scatter.19.cloned.1.call-done = bf16[128,1024]{1,0:T(8,128)(2,1)} async-done(((bf16[512,1024]{1,0:T(8,128)(2,1)}), bf16[128,1024]{1,0:T(8,128)(2,1)}) %reduce-scatter.19.cloned.1.call-update) | async-done | bytes 262160 | tf_op jit(solution)/shard_map/reduce_scatter | solution.py:23
  297.3 27.6 %all-gather.29.cloned.1.call-done = bf16[512,1024]{1,0:T(8,128)(2,1)} async-done(((bf16[128,1024]{1,0:T(8,128)(2,1)}), bf16[512,1024]{1,0:T(8,128)(2,1)}) %all-gather.29.cloned.1.call-update) | async-done | bytes 1048592 | tf_op jit(solution)/shard_map/all_gather | solution.py:19
  326.5 3.5 fusion.131
  330.0 4.8 fusion.146
  334.9 3.0 convolution_convert_fusion.12
  339.6 24.5 %reduce-scatter.21.cloned.1.call-done = bf16[128,1024]{1,0:T(8,128)(2,1)} async-done(((bf16[512,1024]{1,0:T(8,128)(2,1)}), bf16[128,1024]{1,0:T(8,128)(2,1)}) %reduce-scatter.21.cloned.1.call-update) | async-done | bytes 262160 | tf_op jit(solution)/shard_map/reduce_scatter | solution.py:23
  368.0 27.8 %all-gather.31.cloned.1.call-done = bf16[512,1024]{1,0:T(8,128)(2,1)} async-done(((bf16[128,1024]{1,0:T(8,128)(2,1)}), bf16[512,1024]{1,0:T(8,128)(2,1)}) %all-gather.31.cloned.1.call-update) | async-done | bytes 1048592 | tf_op jit(solution)/shard_map/all_gather | solution.py:19
  395.8 4.5 fusion.39
  400.3 27.9 %all-gather.33.cloned.1.call-done = bf16[512,1024]{1,0:T(8,128)(2,1)} async-done(((bf16[512,256]{1,0:T(8,128)(2,1)}), bf16[512,1024]{1,0:T(8,128)(2,1)}) %all-gather.33.cloned.1.call-update) | async-done | bytes 1048592 | tf_op jit(solution)/shard_map/all_gather | solution.py:15
  428.2 5.2 convert_reduce_fusion.2
  434.3 2.3 fusion.45
  436.7 4.8 fusion.44
  441.6 17.7 %reduce-scatter.25.cloned.1.call-done = bf16[128,1024]{1,0:T(8,128)(2,1)} async-done(((bf16[512,1024]{1,0:T(8,128)(2,1)}), bf16[128,1024]{1,0:T(8,128)(2,1)}) %reduce-scatter.25.cloned.1.call-update) | async-done | bytes 262160 | tf_op jit(solution)/shard_map/reduce_scatter | solution.py:23
  460.6 27.2 %reduce-scatter.23.cloned.1.call-done = bf16[128,1024]{1,0:T(8,128)(2,1)} async-done(((bf16[512,1024]{1,0:T(8,128)(2,1)}), bf16[128,1024]{1,0:T(8,128)(2,1)}) %reduce-scatter.23.cloned.1.call-update) | async-done | bytes 262160 | tf_op jit(solution)/shard_map/reduce_scatter | solution.py:23
  487.8 2.3 convert_reduce_fusion.14
  490.3 28.4 %all-gather.35.cloned.1.call-done = bf16[512,1024]{1,0:T(8,128)(2,1)} async-done(((bf16[128,1024]{1,0:T(8,128)(2,1)}), bf16[512,1024]{1,0:T(8,128)(2,1)}) %all-gather.35.cloned.1.call-update) | async-done | bytes 1048592 | tf_op jit(solution)/shard_map/all_gather | solution.py:19
  520.5 3.2 convert_reduce_fusion.12
  528.6 2.0 bitcast_convert_fusion.1
  530.7 24.7 %reduce-scatter.27.cloned.1.call-done = bf16[128,1024]{1,0:T(8,128)(2,1)} async-done(((bf16[512,1024]{1,0:T(8,128)(2,1)}), bf16[128,1024]{1,0:T(8,128)(2,1)}) %reduce-scatter.27.cloned.1.call-update) | async-done | bytes 262160 | tf_op jit(solution)/shard_map/reduce_scatter | solution.py:23
  558.6 28.6 %all-gather.37.cloned.1.call-done = bf16[512,1024]{1,0:T(8,128)(2,1)} async-done(((bf16[128,1024]{1,0:T(8,128)(2,1)}), bf16[512,1024]{1,0:T(8,128)(2,1)}) %all-gather.37.cloned.1.call-update) | async-done | bytes 1048592 | tf_op jit(solution)/shard_map/all_gather | solution.py:19
  587.2 5.2 convert_reduce_fusion.3
  593.4 2.3 fusion.47
  595.7 24.7 %reduce-scatter.29.cloned.1.call-done = bf16[128,1024]{1,0:T(8,128)(2,1)} async-done(((bf16[512,1024]{1,0:T(8,128)(2,1)}), bf16[128,1024]{1,0:T(8,128)(2,1)}) %reduce-scatter.29.cloned.1.call-update) | async-done | bytes 262160 | tf_op jit(solution)/shard_map/reduce_scatter | solution.py:23
  624.4 4.8 convolution_convert_fusion
  629.5 4.8 convolution_convert_fusion.1
  634.4 4.2 convolution_convert_fusion.2
  638.7 4.2 convolution_convert_fusion.3
  643.0 10.0 all-gather.39.cloned.1.call-done
  654.9 3.3 multiply_reduce_fusion
  663.2 2.0 bitcast_convert_fusion
  666.6 2.6 convolution_convert_fusion.7
  673.7 4.0 all-to-all-start
  677.9 6.3 all-to-all-done
  686.9 2.0 maximum_select_fusion
  693.5 35.1 %reduce-scatter.45.cloned.1.call-done = bf16[1024,256]{1,0:T(8,128)(2,1)} async-done(((bf16[1024,1024]{1,0:T(8,128)(2,1)}), bf16[1024,256]{1,0:T(8,128)(2,1)}) %reduce-scatter.45.cloned.1.call-update) | async-done | bytes 524304 | tf_op jit(solution)/shard_map/reduce_scatter | solution.py:282
  728.6 2.0 broadcast_select_fusion
  730.8 36.0 %reduce-scatter.43.cloned.1.call-done = bf16[256,1024]{1,0:T(8,128)(2,1)} async-done(((bf16[1024,1024]{1,0:T(8,128)(2,1)}), bf16[256,1024]{1,0:T(8,128)(2,1)}) %reduce-scatter.43.cloned.1.call-update) | async-done | bytes 524304 | tf_op jit(solution)/shard_map/reduce_scatter | solution.py:282
  766.8 38.0 %reduce-scatter.41.cloned.1.call-done = bf16[256,1024]{1,0:T(8,128)(2,1)} async-done(((bf16[1024,1024]{1,0:T(8,128)(2,1)}), bf16[256,1024]{1,0:T(8,128)(2,1)}) %reduce-scatter.41.cloned.1.call-update) | async-done | bytes 524304 | tf_op jit(solution)/shard_map/reduce_scatter | solution.py:282
  806.1 2.2 add_bitcast_fusion
  808.3 24.6 %reduce-scatter.31.cloned.1.call-done = bf16[128,1024]{1,0:T(8,128)(2,1)} async-done(((bf16[512,1024]{1,0:T(8,128)(2,1)}), bf16[128,1024]{1,0:T(8,128)(2,1)}) %reduce-scatter.31.cloned.1.call-update) | async-done | bytes 262160 | tf_op jit(solution)/shard_map/reduce_scatter | solution.py:23
  836.0 6.0 all-to-all-start.1
  842.0 2.3 add_bitcast_fusion.1
  844.3 17.6 %reduce-scatter.39.cloned.1.call-done = bf16[256,256]{1,0:T(8,128)(2,1)} async-done(((bf16[256,1024]{1,0:T(8,128)(2,1)}), bf16[256,256]{1,0:T(8,128)(2,1)}) %reduce-scatter.39.cloned.1.call-update) | async-done | bytes 131088 | tf_op jit(solution)/shard_map/reduce_scatter | solution.py:282
  861.9 28.5 %reduce-scatter.37.cloned.1.call-done = bf16[256,256]{1,0:T(8,128)(2,1)} async-done(((bf16[256,1024]{1,0:T(8,128)(2,1)}), bf16[256,256]{1,0:T(8,128)(2,1)}) %reduce-scatter.37.cloned.1.call-update) | async-done | bytes 131088 | tf_op jit(solution)/shard_map/reduce_scatter | solution.py:282
  894.1 30.3 %reduce-scatter.35.cloned.1.call-done = bf16[256,4,192]{0,2,1:T(8,128)(2,1)} async-done(((bf16[1024,4,192]{0,2,1:T(8,128)(2,1)}), bf16[256,4,192]{0,2,1:T(8,128)(2,1)}) %reduce-scatter.35.cloned.1.call-update) | async-done | bytes 393232 | tf_op jit(solution)/shard_map/reduce_scatter | solution.py:282
  924.5 34.2 %reduce-scatter.33.cloned.1.call-done = bf16[256,4,192]{0,2,1:T(8,128)(2,1)} async-done(((bf16[1024,4,192]{0,2,1:T(8,128)(2,1)}), bf16[256,4,192]{0,2,1:T(8,128)(2,1)}) %reduce-scatter.33.cloned.1.call-update) | async-done | bytes 393232 | tf_op jit(solution)/shard_map/reduce_scatter | solution.py:282
  960.6 128.7 %all-reduce.3.cloned.1.call-done = f32[32,768]{1,0:T(8,128)} async-done(((f32[32,768]{1,0:T(8,128)}), f32[32,768]{1,0:T(8,128)}) %all-reduce.3.cloned.1.call-update) | async-done | bytes 98320
  1091.4 2.0 dynamic-slice.10
  1093.5 2.1 fusion.139
  (333 shorter events, 73.0 us)
Async XLA Ops:
  7.2 34.6 %copy-start.39 = (bf16[1,4,64,256]{3,2,1,0:T(8,128)(2,1)S(1)}, bf16[1,4,64,256]{3,2,1,0:T(8,128)(2,1)}, u32[]{:S(2)}) copy-start(bf16[1,4,64,256]{3,2,1,0:T(8,128)(2,1)} %param.22) | copy-start | bytes 393220
  7.2 34.5 %all-gather.41.cloned.1.call-start = ((), (), s32[]{:S(2)}) async-start(), calls=%async_computation.42 | async-start | bytes 1966080 | tf_op jit(solution)/shard_map/all_gather | solution.py:240
  7.9 48.3 %copy-start.55 = (bf16[1,4,32]{2,1,0:T(4,128)(2,1)S(1)}, bf16[1,4,32]{2,1,0:T(4,128)(2,1)}, u32[]{:S(2)}) copy-start(bf16[1,4,32]{2,1,0:T(4,128)(2,1)} %param.21) | copy-start | bytes 772
  8.0 48.4 %copy-start.46 = (bf16[1,256]{1,0:T(2,128)(2,1)S(1)}, bf16[1,256]{1,0:T(2,128)(2,1)}, u32[]{:S(2)}) copy-start(bf16[1,256]{1,0:T(2,128)(2,1)} %param.27) | copy-start | bytes 1540
  8.0 48.4 %copy-start.47 = (bf16[1,64]{1,0:T(2,128)(2,1)S(1)}, bf16[1,64]{1,0:T(2,128)(2,1)}, u32[]{:S(2)}) copy-start(bf16[1,64]{1,0:T(2,128)(2,1)} %param.18) | copy-start | bytes 388
  8.0 48.4 %copy-start.48 = (bf16[1,64]{1,0:T(2,128)(2,1)S(1)}, bf16[1,64]{1,0:T(2,128)(2,1)}, u32[]{:S(2)}) copy-start(bf16[1,64]{1,0:T(2,128)(2,1)} %param.19) | copy-start | bytes 388
  8.0 48.4 %copy-start.49 = (bf16[1,64]{1,0:T(2,128)(2,1)S(1)}, bf16[1,64]{1,0:T(2,128)(2,1)}, u32[]{:S(2)}) copy-start(bf16[1,64]{1,0:T(2,128)(2,1)} %param.23) | copy-start | bytes 388
  8.0 48.4 %copy-start.50 = (bf16[1,64]{1,0:T(2,128)(2,1)S(1)}, bf16[1,64]{1,0:T(2,128)(2,1)}, u32[]{:S(2)}) copy-start(bf16[1,64]{1,0:T(2,128)(2,1)} %param.24) | copy-start | bytes 388
  8.0 48.4 %copy-start.51 = (bf16[1,64]{1,0:T(2,128)(2,1)S(1)}, bf16[1,64]{1,0:T(2,128)(2,1)}, u32[]{:S(2)}) copy-start(bf16[1,64]{1,0:T(2,128)(2,1)} %param.25) | copy-start | bytes 388
  8.0 48.4 %copy-start.52 = (bf16[1,64]{1,0:T(2,128)(2,1)S(1)}, bf16[1,64]{1,0:T(2,128)(2,1)}, u32[]{:S(2)}) copy-start(bf16[1,64]{1,0:T(2,128)(2,1)} %param.29) | copy-start | bytes 388
  8.0 111.8 %all-gather.25.cloned.1.call-start = ((), (), s32[]{:S(2)}) async-start(), calls=%async_computation.18 | async-start | bytes 1310720 | tf_op jit(solution)/shard_map/all_gather | solution.py:15
  9.0 112.6 %all-gather.43.cloned.1.call-start = ((), (), s32[]{:S(2)}) async-start(), calls=%async_computation.43 | async-start | bytes 4718592 | tf_op jit(solution)/shard_map/all_gather | solution.py:241
  41.7 77.8 %copy-start.45 = (s32[2,512]{1,0:T(2,128)S(1)}, s32[2,512]{1,0:T(2,128)}, u32[]{:S(2)}) copy-start(s32[2,512]{1,0:T(2,128)} %param.16) | copy-start | bytes 12292
  41.8 92.7 %all-gather.45.cloned.1.call-start = ((), (), s32[]{:S(2)}) async-start(), calls=%async_computation.44 | async-start | bytes 1572864 | tf_op jit(solution)/shard_map/all_gather | solution.py:241
  55.6 82.2 %all-gather.47.cloned.1.call-start = ((), (), s32[]{:S(2)}) async-start(), calls=%async_computation.45 | async-start | bytes 2621440 | tf_op jit(solution)/shard_map/all_gather | solution.py:240
  56.2 108.2 %reduce-scatter.17.cloned.1.call-start = ((), (), s32[]{:S(2)}) async-start(), calls=%async_computation.19 | async-start | bytes 1310720 | tf_op jit(solution)/shard_map/reduce_scatter | solution.py:23
  137.0 64.9 %all-gather.51.cloned.1.call-start = ((), (), s32[]{:S(2)}) async-start(), calls=%async_computation.47 | async-start | bytes 2621440 | tf_op jit(solution)/shard_map/all_gather | solution.py:240
  137.8 79.6 %all-gather.49.cloned.1.call-start = ((), (), s32[]{:S(2)}) async-start(), calls=%async_computation.46 | async-start | bytes 6291456 | tf_op jit(solution)/shard_map/all_gather | solution.py:241
  138.5 109.9 %all-gather.27.cloned.1.call-start = ((), (), s32[]{:S(2)}) async-start(), calls=%async_computation.20 | async-start | bytes 1310720 | tf_op jit(solution)/shard_map/all_gather | solution.py:19
  167.4 95.8 %all-gather.53.cloned.1.call-start = ((), (), s32[]{:S(2)}) async-start(), calls=%async_computation.48 | async-start | bytes 6291456 | tf_op jit(solution)/shard_map/all_gather | solution.py:241
  201.9 92.4 %reduce-scatter.19.cloned.1.call-start = ((), (), s32[]{:S(2)}) async-start(), calls=%async_computation.21 | async-start | bytes 1310720 | tf_op jit(solution)/shard_map/reduce_scatter | solution.py:23
  263.2 31.1 %copy-start.4 = (bf16[128,1024]{1,0:T(8,128)(2,1)S(1)}, bf16[128,1024]{1,0:T(8,128)(2,1)}, u32[]{:S(2)}) copy-start(bf16[128,1024]{1,0:T(8,128)(2,1)} %reduce-scatter.17.cloned.1.call-done) | copy-start | bytes 786436
  268.0 56.8 %all-gather.29.cloned.1.call-start = ((), (), s32[]{:S(2)}) async-start(), calls=%async_computation.22 | async-start | bytes 1310720 | tf_op jit(solution)/shard_map/all_gather | solution.py:19
  296.1 68.0 %reduce-scatter.21.cloned.1.call-start = ((), (), s32[]{:S(2)}) async-start(), calls=%async_computation.23 | async-start | bytes 1310720 | tf_op jit(solution)/shard_map/reduce_scatter | solution.py:23
  297.3 37.6 %copy-start.41 = (f32[4,64]{1,0:T(4,128)}, f32[4,64]{1,0:T(4,128)S(1)}, u32[]{:S(2)}) copy-start(f32[4,64]{1,0:T(4,128)S(1)} %get-tuple-element.81) | copy-start | bytes 3076
  337.8 29.3 %copy-start.21 = (bf16[4,64,512]{2,1,0:T(8,128)(2,1)}, bf16[4,64,512]{2,1,0:T(8,128)(2,1)S(1)}, u32[]{:S(2)}) copy-start(bf16[4,64,512]{2,1,0:T(8,128)(2,1)S(1)} %convolution_convert_fusion.12) | copy-start | bytes 786436
  337.8 29.3 %copy-start.40 = (bf16[1024,256]{1,0:T(8,128)(2,1)S(1)}, bf16[1024,256]{1,0:T(8,128)(2,1)}, u32[]{:S(2)}) copy-start(bf16[1024,256]{1,0:T(8,128)(2,1)} %param.17) | copy-start | bytes 1572868
  339.3 56.5 %all-gather.31.cloned.1.call-start = ((), (), s32[]{:S(2)}) async-start(), calls=%async_computation.24 | async-start | bytes 1310720 | tf_op jit(solution)/shard_map/all_gather | solution.py:19
  367.1 61.1 %all-gather.33.cloned.1.call-start = ((), (), s32[]{:S(2)}) async-start(), calls=%async_computation.26 | async-start | bytes 1310720 | tf_op jit(solution)/shard_map/all_gather | solution.py:15
  367.9 91.3 %reduce-scatter.25.cloned.1.call-start = ((), (), s32[]{:S(2)}) async-start(), calls=%async_computation.27 | async-start | bytes 1310720 | tf_op jit(solution)/shard_map/reduce_scatter | solution.py:23
  436.6 51.2 %reduce-scatter.23.cloned.1.call-start = ((), (), s32[]{:S(2)}) async-start(), calls=%async_computation.25 | async-start | bytes 1310720 | tf_op jit(solution)/shard_map/reduce_scatter | solution.py:23
  441.5 77.3 %all-gather.35.cloned.1.call-start = ((), (), s32[]{:S(2)}) async-start(), calls=%async_computation.28 | async-start | bytes 1310720 | tf_op jit(solution)/shard_map/all_gather | solution.py:19
  490.1 65.3 %reduce-scatter.27.cloned.1.call-start = ((), (), s32[]{:S(2)}) async-start(), calls=%async_computation.29 | async-start | bytes 1310720 | tf_op jit(solution)/shard_map/reduce_scatter | solution.py:23
  530.6 56.6 %all-gather.37.cloned.1.call-start = ((), (), s32[]{:S(2)}) async-start(), calls=%async_computation.30 | async-start | bytes 1310720 | tf_op jit(solution)/shard_map/all_gather | solution.py:19
  558.6 61.9 %reduce-scatter.29.cloned.1.call-start = ((), (), s32[]{:S(2)}) async-start(), calls=%async_computation.31 | async-start | bytes 1310720 | tf_op jit(solution)/shard_map/reduce_scatter | solution.py:23
  593.4 29.0 %copy-start.10 = (bf16[128,1024]{1,0:T(8,128)(2,1)S(1)}, bf16[128,1024]{1,0:T(8,128)(2,1)}, u32[]{:S(2)}) copy-start(bf16[128,1024]{1,0:T(8,128)(2,1)} %get-tuple-element.45) | copy-start | bytes 786436
  595.7 57.3 %all-gather.39.cloned.1.call-start = ((), (), s32[]{:S(2)}) async-start(), calls=%async_computation.32 | async-start | bytes 1310720 | tf_op jit(solution)/shard_map/all_gather | solution.py:19
  624.4 69.2 %reduce-scatter.47.cloned.1.call-start = ((), (), s32[]{:S(2)}) async-start(), calls=%async_computation.41 | async-start | bytes 2621440 | tf_op jit(solution)/shard_map/reduce_scatter | solution.py:282
  629.2 99.4 %reduce-scatter.45.cloned.1.call-start = ((), (), s32[]{:S(2)}) async-start(), calls=%async_computation.40 | async-start | bytes 2621440 | tf_op jit(solution)/shard_map/reduce_scatter | solution.py:282
  634.4 132.4 %reduce-scatter.43.cloned.1.call-start = ((), (), s32[]{:S(2)}) async-start(), calls=%async_computation.39 | async-start | bytes 2621440 | tf_op jit(solution)/shard_map/reduce_scatter | solution.py:282
  638.6 166.2 %reduce-scatter.41.cloned.1.call-start = ((), (), s32[]{:S(2)}) async-start(), calls=%async_computation.38 | async-start | bytes 2621440 | tf_op jit(solution)/shard_map/reduce_scatter | solution.py:282
  642.9 189.9 %reduce-scatter.31.cloned.1.call-start = ((), (), s32[]{:S(2)}) async-start(), calls=%async_computation.33 | async-start | bytes 1310720 | tf_op jit(solution)/shard_map/reduce_scatter | solution.py:23
  665.2 196.7 %reduce-scatter.39.cloned.1.call-start = ((), (), s32[]{:S(2)}) async-start(), calls=%async_computation.37 | async-start | bytes 655360 | tf_op jit(solution)/shard_map/reduce_scatter | solution.py:282
  666.5 223.9 %reduce-scatter.37.cloned.1.call-start = ((), (), s32[]{:S(2)}) async-start(), calls=%async_computation.36 | async-start | bytes 655360 | tf_op jit(solution)/shard_map/reduce_scatter | solution.py:282
  669.2 255.2 %reduce-scatter.35.cloned.1.call-start = ((), (), s32[]{:S(2)}) async-start(), calls=%async_computation.35 | async-start | bytes 1966080 | tf_op jit(solution)/shard_map/reduce_scatter | solution.py:282
  673.7 10.6 all-to-all-start
  677.6 281.0 %reduce-scatter.33.cloned.1.call-start = ((), (), s32[]{:S(2)}) async-start(), calls=%async_computation.34 | async-start | bytes 1966080 | tf_op jit(solution)/shard_map/reduce_scatter | solution.py:282
  685.1 1.7 collective-permute-start
  693.5 112.5 %copy-start.13 = (bf16[1024,256]{1,0:T(8,128)(2,1)S(1)}, bf16[1024,256]{1,0:T(8,128)(2,1)}, u32[]{:S(2)}) copy-start(bf16[1024,256]{1,0:T(8,128)(2,1)} %reduce-scatter.47.cloned.1.call-done) | copy-start | bytes 1572868
  728.6 77.4 %copy-start.14 = (bf16[1024,256]{1,0:T(8,128)(2,1)S(1)}, bf16[1024,256]{1,0:T(8,128)(2,1)}, u32[]{:S(2)}) copy-start(bf16[1024,256]{1,0:T(8,128)(2,1)} %reduce-scatter.45.cloned.1.call-done) | copy-start | bytes 1572868
  730.6 75.4 %collective-permute-start.5 = (bf16[1024,256]{1,0:T(8,128)(2,1)}, bf16[1024,256]{1,0:T(8,128)(2,1)}, u32[]{:S(2)}, u32[]{:S(2)}) collective-permute-start(bf16[1024,256]{1,0:T(8,128)(2,1)} %broadcast_select_fusion), channel_id=1, source_target_pairs={{0,16},{16,0},{1,17},{17,1},{2,18},{18,2},{3,19},{19,3},{4,20},{20... | collective-permute-start | bytes 1572872 | tf_op jit(solution)/shard_map/ppermute | solution.py:179
  806.0 36.1 %collective-permute-start.4 = (bf16[256,1024]{1,0:T(8,128)(2,1)S(1)}, bf16[256,1024]{1,0:T(8,128)(2,1)}, u32[]{:S(2)}, u32[]{:S(2)}) collective-permute-start(bf16[256,1024]{1,0:T(8,128)(2,1)S(1)} %broadcast_select_fusion.1), channel_id=1, source_target_pairs={{0,16},{16,0},{1,17},{17,1},{2,18},{18,2},{3,19},{19,3},{4,20},{20... | collective-permute-start | bytes 1572872 | tf_op jit(solution)/shard_map/ppermute | solution.py:179
  808.3 33.8 %copy-start.11 = (bf16[256,1024]{1,0:T(8,128)(2,1)S(1)}, bf16[256,1024]{1,0:T(8,128)(2,1)}, u32[]{:S(2)}) copy-start(bf16[256,1024]{1,0:T(8,128)(2,1)} %reduce-scatter.43.cloned.1.call-done) | copy-start | bytes 1572868
  808.3 33.8 %copy-start.12 = (bf16[256,1024]{1,0:T(8,128)(2,1)S(1)}, bf16[256,1024]{1,0:T(8,128)(2,1)}, u32[]{:S(2)}) copy-start(bf16[256,1024]{1,0:T(8,128)(2,1)} %reduce-scatter.41.cloned.1.call-done) | copy-start | bytes 1572868
  836.0 56.5 %all-to-all-start.1 = ((bf16[128,4,256]{2,0,1:T(8,128)(2,1)}), bf16[128,4,256]{2,0,1:T(8,128)(2,1)S(1)}, u32[]{:S(2)}, u32[]{:S(2)}) async-start(bf16[128,4,256]{2,0,1:T(8,128)(2,1)} %bitcast.186), calls=%async_computation.9 | async-start | bytes 524288 | tf_op jit(solution)/shard_map/all_to_all | solution.py:293
  842.0 247.3 %all-reduce.3.cloned.1.call-start = ((), (), s32[]{:S(2)}) async-start(), calls=%async_computation.49 | async-start | bytes 196608
  861.9 97.9 %copy-start.35 = (bf16[256,256]{1,0:T(8,128)(2,1)S(1)}, bf16[256,256]{1,0:T(8,128)(2,1)}, u32[]{:S(2)}) copy-start(bf16[256,256]{1,0:T(8,128)(2,1)} %reduce-scatter.39.cloned.1.call-done) | copy-start | bytes 393220
  890.5 69.4 %copy-start.36 = (bf16[256,256]{1,0:T(8,128)(2,1)S(1)}, bf16[256,256]{1,0:T(8,128)(2,1)}, u32[]{:S(2)}) copy-start(bf16[256,256]{1,0:T(8,128)(2,1)} %reduce-scatter.37.cloned.1.call-done) | copy-start | bytes 393220
  891.4 68.4 %collective-permute-start.3 = (bf16[256,256]{1,0:T(8,128)(2,1)S(1)}, bf16[256,256]{1,0:T(8,128)(2,1)S(1)}, u32[]{:S(2)}, u32[]{:S(2)}) collective-permute-start(bf16[256,256]{1,0:T(8,128)(2,1)S(1)} %broadcast_select_fusion.3), channel_id=1, source_target_pairs={{0,16},{16,0},{1,17},{17,1},{2,18},{18,2},{3,19},{19,3},{4,20},{20... | collective-permute-start | bytes 393224 | tf_op jit(solution)/shard_map/ppermute | solution.py:179
  893.6 202.0 %collective-permute-start.1 = (bf16[512,256]{1,0:T(8,128)(2,1)S(1)}, bf16[512,256]{1,0:T(8,128)(2,1)S(1)}, u32[]{:S(2)}, u32[]{:S(2)}) collective-permute-start(bf16[512,256]{1,0:T(8,128)(2,1)S(1)} %get-tuple-element.55), channel_id=1, source_target_pairs={{0,16},{16,0},{1,17},{17,1},{2,18},{18,2},{3,19},{19,3},{4,20},{20... | collective-permute-start | bytes 786440 | tf_op jit(solution)/shard_map/ppermute | solution.py:179
  924.5 172.2 %copy-start.16 = (bf16[256,4,192]{0,2,1:T(8,128)(2,1)S(1)}, bf16[256,4,192]{0,2,1:T(8,128)(2,1)}, u32[]{:S(2)}) copy-start(bf16[256,4,192]{0,2,1:T(8,128)(2,1)} %reduce-scatter.35.cloned.1.call-done) | copy-start | bytes 1179652
  958.6 138.0 %copy-start.17 = (bf16[256,4,192]{0,2,1:T(8,128)(2,1)S(1)}, bf16[256,4,192]{0,2,1:T(8,128)(2,1)}, u32[]{:S(2)}) copy-start(bf16[256,4,192]{0,2,1:T(8,128)(2,1)} %reduce-scatter.33.cloned.1.call-done) | copy-start | bytes 1179652
  958.6 139.1 %copy-start.1 = (bf16[1024,256]{1,0:T(8,128)(2,1)S(1)}, bf16[1024,256]{1,0:T(8,128)(2,1)}, u32[]{:S(2)}) copy-start(bf16[1024,256]{1,0:T(8,128)(2,1)} %param.15) | copy-start | bytes 1572868
  959.7 136.9 %collective-permute-start.2 = (bf16[256,4,192]{0,2,1:T(8,128)(2,1)S(1)}, bf16[256,4,192]{0,2,1:T(8,128)(2,1)S(1)}, u32[]{:S(2)}, u32[]{:S(2)}) collective-permute-start(bf16[256,4,192]{0,2,1:T(8,128)(2,1)S(1)} %broadcast_select_fusion.2), channel_id=1, source_target_pairs={{0,16},{16,0},{1,17},{17,1},{2,18},{18,2},{3,19},{19,3},{4,20},{20... | collective-permute-start | bytes 1179656 | tf_op jit(solution)/shard_map/ppermute | solution.py:179
  (35 other events, 172.1 us)
Sparse Core Ops, SparseCore 0:
  9.8 31.8 all-gather.40
  43.9 31.0 all-gather.24
  76.6 9.6 all-gather.42
  87.6 10.1 all-gather.44
  99.6 36.1 all-gather.46
  138.5 25.9 reduce-scatter.16
  166.3 35.6 all-gather.50
  203.4 13.9 all-gather.48
  219.6 28.8 all-gather.26
  249.8 13.3 all-gather.52
  268.1 26.1 reduce-scatter.18
  296.3 28.4 all-gather.28
  339.4 24.6 reduce-scatter.20
  367.2 28.4 all-gather.30
  397.8 30.3 all-gather.32
  436.8 22.4 reduce-scatter.24
  462.0 25.7 reduce-scatter.22
  490.2 28.4 all-gather.34
  530.7 24.6 reduce-scatter.26
  558.7 28.4 all-gather.36
  595.8 24.6 reduce-scatter.28
  624.5 28.4 all-gather.38
  656.0 34.5 reduce-scatter.46
  693.4 35.1 reduce-scatter.44
  731.6 35.1 reduce-scatter.42
  769.6 35.1 reduce-scatter.40
  807.6 25.2 reduce-scatter.30
  836.2 25.6 reduce-scatter.38
  865.3 25.0 reduce-scatter.36
  893.3 31.1 reduce-scatter.34
  927.4 31.1 reduce-scatter.32
  964.8 124.4 all-reduce.2
where the time goes:
time: 1110 us; the launch traced here: 1100 us
  waiting for transfers between devices  828 us (75%)
  matrix products  101 us (9%)
  blocking collectives  75.8 us (7%)
  other arithmetic  48.3 us (4%)
  local copies, waits for them, and re-layouts  22.2 us (2%)
  between operations  15.5 us (1%)
  starting transfers between devices  13.1 us (1%)
    reduce_scatter x8, waiting for transfers between devices, reduce_big(): lax.psum_scatter(item.astype(bf16), 'seq', scatter_dimension=axis, tiled=...  220 us
    reduce_scatter x8, waiting for transfers between devices, scatter_rows(): lax.psum_scatter(partial_rows.astype(bf16), 'tensor', scatter_dimension=0...  195 us
    all_gather x6, waiting for transfers between devices, gather_rows(): return lax.all_gather(piece, 'tensor', axis=0, tiled=True)  153 us
    unnamed x33, waiting for transfers between devices  132 us
    all_gather x3, waiting for transfers between devices, pair(): gathered = lax.all_gather(weight, 'seq', axis=axis, tiled=True)  67.2 us
    dot_general x18, matrix products, dot(): lax.dot_general(left, right, (dims, ((), ())), preferred_element_type=f32)  62.8 us
    all_gather x1, blocking collectives, body(): lax.all_gather(packed, ('section', 'tensor', 'seq'), axis=0, tiled=False)  62.1 us
    all_gather x2, waiting for transfers between devices, gather_columns(): return lax.all_gather(piece, 'tensor', axis=1, tiled=True)  27.9 us
  transfers between devices with their start and end apart: 40, of which 29 were waited for; matrix products, arithmetic and copies ran while one was open for 10% of the time, Pallas kernels for 0%

commit v1 on v0

--- a/solution.py
+++ b/solution.py
@@ -11,12 +11,29 @@
 bf16 = jnp.bfloat16
 
 
+def laid_out(blocks, dim):
+    blocks = jnp.moveaxis(blocks, 0, dim)
+    dims = blocks.shape
+    return blocks.reshape(*dims[:dim], dims[dim] * dims[dim + 1], *dims[dim + 2 :])
+
+
+def ring_gather(x, axis, dim):
+    size = lax.axis_size(axis)
+    right = [(i, (i + 1) % size) for i in range(size)]
+    tiles = [x]
+    while len(tiles) < size:
+        tiles.append(lax.ppermute(tiles[-1], axis, right))
+    position = lax.axis_index(axis)
+    tiles = jnp.stack(tiles)[(position - jnp.arange(size)) % size]
+    return laid_out(tiles, dim)
+
+
 def gather_columns(piece):
     return lax.all_gather(piece, "tensor", axis=1, tiled=True)
 
 
 def gather_rows(piece):
-    return lax.all_gather(piece, "tensor", axis=0, tiled=True)
+    return ring_gather(piece, "tensor", 0)
 
 
 def scatter_rows(partial_rows):

time: 1110 us -> 1050 us (0.946)
  waiting for transfers between devices: 828 us -> 721 us
  starting transfers between devices: 13.1 us -> 40.3 us
  local copies, waits for them, and re-layouts: 22.2 us -> 36.4 us
    all_gather x6 -> x0, waiting for transfers between devices: 153 us -> none  [gather_rows(): return lax.all_gather(piece, 'tensor', axis=0, tiled=True)]
    ppermute x0 -> x18, waiting for transfers between devices: none -> 136 us  [ring_gather(): tiles.append(lax.ppermute(tiles[-1], axis, right))]
    reduce_scatter x8, waiting for transfers between devices: 220 us -> 169 us  [reduce_big(): lax.psum_scatter(item.astype(bf16), 'seq', scatter_dimension=axis, tiled=...]
    all_gather x2, waiting for transfers between devices: 27.9 us -> 0.02 us  [gather_columns(): return lax.all_gather(piece, 'tensor', axis=1, tiled=True)]
    all_gather x4, waiting for transfers between devices: 25.7 us -> 0.07 us  [pair(): return lax.all_gather(gathered, 'section', axis=0, tiled=False)]
    ppermute x0 -> x18, starting transfers between devices: none -> 25.4 us  [ring_gather(): tiles.append(lax.ppermute(tiles[-1], axis, right))]
    reduce_scatter x8, waiting for transfers between devices: 195 us -> 208 us  [scatter_rows(): lax.psum_scatter(partial_rows.astype(bf16), 'tensor', scatter_dimension=0...]
    gather x0 -> x6, local copies, waits for them, and re-layouts: none -> 11.5 us  [ring_gather(): tiles = jnp.stack(tiles)[(position - jnp.arange(size)) % size]]
  transfers between devices with their start and end apart: 40 -> 52, of which waited for: 29 -> 39; matrix products, arithmetic and copies ran while one was open for 10% -> 11% of each run, Pallas kernels for 0% -> 0%
where the time goes in v1:
time: 1050 us; the launch traced here: 1040 us
  waiting for transfers between devices  721 us (69%)
  matrix products  96.3 us (9%)
  blocking collectives  75.9 us (7%)
  other arithmetic  51.7 us (5%)
  starting transfers between devices  40.3 us (4%)
  local copies, waits for them, and re-layouts  36.4 us (3%)
  between operations  15.3 us (1%)
    reduce_scatter x8, waiting for transfers between devices, scatter_rows(): lax.psum_scatter(partial_rows.astype(bf16), 'tensor', scatter_dimension=0...  208 us
    reduce_scatter x8, waiting for transfers between devices, reduce_big(): lax.psum_scatter(item.astype(bf16), 'seq', scatter_dimension=axis, tiled=...  169 us
    ppermute x18, waiting for transfers between devices, ring_gather(): tiles.append(lax.ppermute(tiles[-1], axis, right))  136 us
    unnamed x27, waiting for transfers between devices  129 us
    all_gather x3, waiting for transfers between devices, pair(): gathered = lax.all_gather(weight, 'seq', axis=axis, tiled=True)  68.5 us
    all_gather x1, blocking collectives, body(): lax.all_gather(packed, ('section', 'tensor', 'seq'), axis=0, tiled=False)  62.1 us
    dot_general x18, matrix products, dot(): lax.dot_general(left, right, (dims, ((), ())), preferred_element_type=f32)  61.8 us
    ppermute x18, starting transfers between devices, ring_gather(): tiles.append(lax.ppermute(tiles[-1], axis, right))  25.4 us
  transfers between devices with their start and end apart: 52, of which 39 were waited for; matrix products, arithmetic and copies ran while one was open for 11% of the time, Pallas kernels for 0%

profile of v1, /device:TPU:8, one launch (start us, length us, event | category | flops | bytes accessed | tf_op | source)
XLA Modules:
  0.0 1037.2 jit_solution(4694766318803074013)
XLA Ops:
  9.1 32.7 %all-gather.23.cloned.1.call-done = bf16[1,1024,4,192]{1,3,2,0:T(8,128)(2,1)} async-done(((bf16[1,256,4,192]{1,3,2,0:T(8,128)(2,1)}), bf16[1,1024,4,192]{1,3,2,0:T(8,128)(2,1)}) %all-gather.23.cloned.1.call-update) | async-done | bytes 1572880 | tf_op jit(solution)/shard_map/all_gather | solution.py:257
  41.8 13.8 %all_gather.54 = bf16[256,1024]{1,0:T(8,128)(2,1)} all-gather(bf16[256,256]{1,0:T(8,128)(2,1)S(1)} %bitcast.290), channel_id=1, replica_groups=mesh['section'=2,'seq'=4,'tensor'=4] {'seq'}, dimensions={1}, use_global_device_ids=true | all-gather | bytes 655360 | tf_op jit(solution)/shard_map/all_gather | solution.py:257
  57.1 62.1 %all-gather.8 = bf16[32,1,768]{2,1,0:T(2,128)(2,1)S(1)} all-gather(bf16[1,1,768]{2,1,0:T(2,128)(2,1)S(1)} %reshape.958), channel_id=2, replica_groups=mesh['section'=2,'seq'=4,'tensor'=4] {'section','tensor','seq'}, dimensions={0}, use_global_device_ids=true | all-gather | bytes 50688 | tf_op jit(solution)/shard_map/all_gather | solution.py:253
  122.2 3.6 fusion.136
  127.1 3.7 fusion.143
  130.7 2.7 convolution_convert_fusion.13
  133.5 2.5 convolution_convert_fusion.5
  136.8 35.8 %all-gather.33.cloned.1.call-done = bf16[1,1024,1024]{2,1,0:T(8,128)(2,1)} async-done(((bf16[1,1024,256]{2,1,0:T(8,128)(2,1)}), bf16[1,1024,1024]{2,1,0:T(8,128)(2,1)}) %all-gather.33.cloned.1.call-update) | async-done | bytes 2097168 | tf_op jit(solution)/shard_map/all_gather | solution.py:257
  172.9 27.8 %reduce-scatter.17.cloned.1.call-done = bf16[128,1024]{1,0:T(8,128)(2,1)} async-done(((bf16[512,1024]{1,0:T(8,128)(2,1)}), bf16[128,1024]{1,0:T(8,128)(2,1)}) %reduce-scatter.17.cloned.1.call-update) | async-done | bytes 262160 | tf_op jit(solution)/shard_map/reduce_scatter | solution.py:40
  205.1 6.5 collective-permute-done
  213.1 7.1 collective-permute-done.1
  220.9 7.2 collective-permute-done.2
  228.9 4.9 fusion.35
  233.8 4.8 fusion.46
  238.7 26.4 %reduce-scatter.19.cloned.1.call-done = bf16[128,1024]{1,0:T(8,128)(2,1)} async-done(((bf16[512,1024]{1,0:T(8,128)(2,1)}), bf16[128,1024]{1,0:T(8,128)(2,1)}) %reduce-scatter.19.cloned.1.call-update) | async-done | bytes 262160 | tf_op jit(solution)/shard_map/reduce_scatter | solution.py:40
  268.3 6.5 collective-permute-done.3
  276.4 6.9 collective-permute-done.4
  284.0 7.4 collective-permute-done.5
  297.9 4.8 fusion.144
  302.7 3.0 convolution_convert_fusion.12
  309.0 25.7 %reduce-scatter.21.cloned.1.call-done = bf16[128,1024]{1,0:T(8,128)(2,1)} async-done(((bf16[512,1024]{1,0:T(8,128)(2,1)}), bf16[128,1024]{1,0:T(8,128)(2,1)}) %reduce-scatter.21.cloned.1.call-update) | async-done | bytes 262160 | tf_op jit(solution)/shard_map/reduce_scatter | solution.py:40
  339.1 6.4 collective-permute-done.6
  347.1 14.3 %collective-permute-done.7 = bf16[128,1024]{1,0:T(8,128)(2,1)S(1)} collective-permute-done((bf16[128,1024]{1,0:T(8,128)(2,1)S(1)}, bf16[128,1024]{1,0:T(8,128)(2,1)S(1)}, u32[]{:S(2)}, u32[]{:S(2)}) %collective-permute-start.7) | collective-permute-done | bytes 262176 | tf_op jit(solution)/shard_map/ppermute | solution.py:25
  361.3 2.5 collective-permute-start.8
  363.8 11.2 %collective-permute-done.8 = bf16[128,1024]{1,0:T(8,128)(2,1)S(1)} collective-permute-done((bf16[128,1024]{1,0:T(8,128)(2,1)S(1)}, bf16[128,1024]{1,0:T(8,128)(2,1)S(1)}, u32[]{:S(2)}, u32[]{:S(2)}) %collective-permute-start.8) | collective-permute-done | bytes 262176 | tf_op jit(solution)/shard_map/ppermute | solution.py:25
  376.2 2.8 gather_fusion.2
  379.0 4.5 fusion.39
  383.5 5.2 convert_reduce_fusion.2
  389.7 2.3 fusion.45
  392.0 4.8 fusion.44
  397.1 20.7 %reduce-scatter.25.cloned.1.call-done = bf16[128,1024]{1,0:T(8,128)(2,1)} async-done(((bf16[512,1024]{1,0:T(8,128)(2,1)}), bf16[128,1024]{1,0:T(8,128)(2,1)}) %reduce-scatter.25.cloned.1.call-update) | async-done | bytes 262160 | tf_op jit(solution)/shard_map/reduce_scatter | solution.py:40
  419.2 26.6 %reduce-scatter.23.cloned.1.call-done = bf16[128,1024]{1,0:T(8,128)(2,1)} async-done(((bf16[512,1024]{1,0:T(8,128)(2,1)}), bf16[128,1024]{1,0:T(8,128)(2,1)}) %reduce-scatter.23.cloned.1.call-update) | async-done | bytes 262160 | tf_op jit(solution)/shard_map/reduce_scatter | solution.py:40
  450.0 6.5 collective-permute-done.10
  458.0 7.0 collective-permute-done.11
  465.2 7.8 collective-permute-done.12
  474.1 2.8 gather_fusion.3
  478.7 3.2 convert_reduce_fusion.12
  488.9 26.7 %reduce-scatter.27.cloned.1.call-done = bf16[128,1024]{1,0:T(8,128)(2,1)} async-done(((bf16[512,1024]{1,0:T(8,128)(2,1)}), bf16[128,1024]{1,0:T(8,128)(2,1)}) %reduce-scatter.27.cloned.1.call-update) | async-done | bytes 262160 | tf_op jit(solution)/shard_map/reduce_scatter | solution.py:40
  520.3 6.5 collective-permute-done.13
  528.3 7.1 collective-permute-done.14
  535.4 7.8 collective-permute-done.15
  545.0 5.2 convert_reduce_fusion.3
  553.5 26.7 %reduce-scatter.29.cloned.1.call-done = bf16[128,1024]{1,0:T(8,128)(2,1)} async-done(((bf16[512,1024]{1,0:T(8,128)(2,1)}), bf16[128,1024]{1,0:T(8,128)(2,1)}) %reduce-scatter.29.cloned.1.call-update) | async-done | bytes 262160 | tf_op jit(solution)/shard_map/reduce_scatter | solution.py:40
  587.3 5.3 collective-permute-done.16
  594.2 7.0 collective-permute-done.17
  601.7 7.8 collective-permute-done.18
  614.8 4.8 convolution_convert_fusion
  619.7 4.8 convolution_convert_fusion.1
  624.6 4.2 convolution_convert_fusion.2
  628.9 4.2 convolution_convert_fusion.3
  634.8 3.3 multiply_reduce_fusion
  649.5 7.2 all-to-all-start
  656.9 6.0 all-to-all-done
  674.3 5.7 reduce-scatter.47.cloned.1.call-done
  680.1 38.1 %reduce-scatter.45.cloned.1.call-done = bf16[1024,256]{1,0:T(8,128)(2,1)} async-done(((bf16[1024,1024]{1,0:T(8,128)(2,1)}), bf16[1024,256]{1,0:T(8,128)(2,1)}) %reduce-scatter.45.cloned.1.call-update) | async-done | bytes 524304 | tf_op jit(solution)/shard_map/reduce_scatter | solution.py:299
  720.0 36.3 %reduce-scatter.43.cloned.1.call-done = bf16[256,1024]{1,0:T(8,128)(2,1)} async-done(((bf16[1024,1024]{1,0:T(8,128)(2,1)}), bf16[256,1024]{1,0:T(8,128)(2,1)}) %reduce-scatter.43.cloned.1.call-update) | async-done | bytes 524304 | tf_op jit(solution)/shard_map/reduce_scatter | solution.py:299
  756.3 38.2 %reduce-scatter.41.cloned.1.call-done = bf16[256,1024]{1,0:T(8,128)(2,1)} async-done(((bf16[1024,1024]{1,0:T(8,128)(2,1)}), bf16[256,1024]{1,0:T(8,128)(2,1)}) %reduce-scatter.41.cloned.1.call-update) | async-done | bytes 524304 | tf_op jit(solution)/shard_map/reduce_scatter | solution.py:299
  795.7 26.9 %reduce-scatter.31.cloned.1.call-done = bf16[128,1024]{1,0:T(8,128)(2,1)} async-done(((bf16[512,1024]{1,0:T(8,128)(2,1)}), bf16[128,1024]{1,0:T(8,128)(2,1)}) %reduce-scatter.31.cloned.1.call-update) | async-done | bytes 262160 | tf_op jit(solution)/shard_map/reduce_scatter | solution.py:40
  825.8 6.0 all-to-all-start.1
  835.0 3.7 all-to-all-done.1
  840.5 16.7 %reduce-scatter.35.cloned.1.call-done = bf16[256,4,192]{0,2,1:T(8,128)(2,1)} async-done(((bf16[1024,4,192]{0,2,1:T(8,128)(2,1)}), bf16[256,4,192]{0,2,1:T(8,128)(2,1)}) %reduce-scatter.35.cloned.1.call-update) | async-done | bytes 393232 | tf_op jit(solution)/shard_map/reduce_scatter | solution.py:299
  857.2 34.1 %reduce-scatter.33.cloned.1.call-done = bf16[256,4,192]{0,2,1:T(8,128)(2,1)} async-done(((bf16[1024,4,192]{0,2,1:T(8,128)(2,1)}), bf16[256,4,192]{0,2,1:T(8,128)(2,1)}) %reduce-scatter.33.cloned.1.call-update) | async-done | bytes 393232 | tf_op jit(solution)/shard_map/reduce_scatter | solution.py:299
  893.2 2.4 add_bitcast_fusion.1
  895.5 125.8 %all-reduce.3.cloned.1.call-done = f32[32,768]{1,0:T(8,128)} async-done(((f32[32,768]{1,0:T(8,128)}), f32[32,768]{1,0:T(8,128)}) %all-reduce.3.cloned.1.call-update) | async-done | bytes 98320
  (376 shorter events, 129.1 us)
Async XLA Ops:
  7.2 34.5 %all-gather.23.cloned.1.call-start = ((), (), s32[]{:S(2)}) async-start(), calls=%async_computation.36 | async-start | bytes 1966080 | tf_op jit(solution)/shard_map/all_gather | solution.py:257
  7.9 112.5 %all-gather.19.cloned.1.call-start = ((), (), s32[]{:S(2)}) async-start(), calls=%async_computation.18 | async-start | bytes 1310720 | tf_op jit(solution)/shard_map/all_gather | solution.py:32
  9.0 48.0 %copy-start.54 = (bf16[1,64]{1,0:T(2,128)(2,1)S(1)}, bf16[1,64]{1,0:T(2,128)(2,1)}, u32[]{:S(2)}) copy-start(bf16[1,64]{1,0:T(2,128)(2,1)} %param.23) | copy-start | bytes 388
  9.0 48.0 %copy-start.55 = (bf16[1,64]{1,0:T(2,128)(2,1)S(1)}, bf16[1,64]{1,0:T(2,128)(2,1)}, u32[]{:S(2)}) copy-start(bf16[1,64]{1,0:T(2,128)(2,1)} %param.24) | copy-start | bytes 388
  9.0 48.0 %copy-start.56 = (bf16[1,64]{1,0:T(2,128)(2,1)S(1)}, bf16[1,64]{1,0:T(2,128)(2,1)}, u32[]{:S(2)}) copy-start(bf16[1,64]{1,0:T(2,128)(2,1)} %param.25) | copy-start | bytes 388
  9.0 113.1 %all-gather.25.cloned.1.call-start = ((), (), s32[]{:S(2)}) async-start(), calls=%async_computation.37 | async-start | bytes 4718592 | tf_op jit(solution)/shard_map/all_gather | solution.py:258
  41.7 78.4 %copy-start.50 = (s32[2,512]{1,0:T(2,128)S(1)}, s32[2,512]{1,0:T(2,128)}, u32[]{:S(2)}) copy-start(s32[2,512]{1,0:T(2,128)} %param.16) | copy-start | bytes 12292
  41.8 91.7 %all-gather.27.cloned.1.call-start = ((), (), s32[]{:S(2)}) async-start(), calls=%async_computation.38 | async-start | bytes 1572864 | tf_op jit(solution)/shard_map/all_gather | solution.py:258
  55.6 80.5 %all-gather.29.cloned.1.call-start = ((), (), s32[]{:S(2)}) async-start(), calls=%async_computation.39 | async-start | bytes 2621440 | tf_op jit(solution)/shard_map/all_gather | solution.py:257
  56.2 116.4 %all-gather.33.cloned.1.call-start = ((), (), s32[]{:S(2)}) async-start(), calls=%async_computation.41 | async-start | bytes 2621440 | tf_op jit(solution)/shard_map/all_gather | solution.py:257
  56.8 144.0 %reduce-scatter.17.cloned.1.call-start = ((), (), s32[]{:S(2)}) async-start(), calls=%async_computation.19 | async-start | bytes 1310720 | tf_op jit(solution)/shard_map/reduce_scatter | solution.py:40
  136.0 92.8 %all-gather.31.cloned.1.call-start = ((), (), s32[]{:S(2)}) async-start(), calls=%async_computation.40 | async-start | bytes 6291456 | tf_op jit(solution)/shard_map/all_gather | solution.py:258
  136.8 97.0 %all-gather.35.cloned.1.call-start = ((), (), s32[]{:S(2)}) async-start(), calls=%async_computation.42 | async-start | bytes 6291456 | tf_op jit(solution)/shard_map/all_gather | solution.py:258
  172.7 92.4 %reduce-scatter.19.cloned.1.call-start = ((), (), s32[]{:S(2)}) async-start(), calls=%async_computation.20 | async-start | bytes 1310720 | tf_op jit(solution)/shard_map/reduce_scatter | solution.py:40
  203.0 8.6 collective-permute-start
  211.6 8.6 collective-permute-start.1
  220.2 7.9 collective-permute-start.2
  238.6 96.1 %reduce-scatter.21.cloned.1.call-start = ((), (), s32[]{:S(2)}) async-start(), calls=%async_computation.21 | async-start | bytes 1310720 | tf_op jit(solution)/shard_map/reduce_scatter | solution.py:40
  266.2 8.6 collective-permute-start.3
  274.7 8.6 collective-permute-start.4
  283.3 8.0 collective-permute-start.5
  307.9 75.6 %all-gather.21.cloned.1.call-start = ((), (), s32[]{:S(2)}) async-start(), calls=%async_computation.23 | async-start | bytes 1310720 | tf_op jit(solution)/shard_map/all_gather | solution.py:32
  308.7 109.2 %reduce-scatter.25.cloned.1.call-start = ((), (), s32[]{:S(2)}) async-start(), calls=%async_computation.24 | async-start | bytes 1310720 | tf_op jit(solution)/shard_map/reduce_scatter | solution.py:40
  337.0 8.6 collective-permute-start.6
  345.5 15.8 %collective-permute-start.7 = (bf16[128,1024]{1,0:T(8,128)(2,1)S(1)}, bf16[128,1024]{1,0:T(8,128)(2,1)S(1)}, u32[]{:S(2)}, u32[]{:S(2)}) collective-permute-start(bf16[128,1024]{1,0:T(8,128)(2,1)S(1)} %collective-permute-done.6), channel_id=1, source_target_pairs={{0,1},{1,2},{2,3},{3,0},{4,5},{5,6},{6,7},{7,4},{8,9},{9,10},{10,1... | collective-permute-start | bytes 786440 | tf_op jit(solution)/shard_map/ppermute | solution.py:25
  361.3 13.7 %collective-permute-start.8 = (bf16[128,1024]{1,0:T(8,128)(2,1)S(1)}, bf16[128,1024]{1,0:T(8,128)(2,1)S(1)}, u32[]{:S(2)}, u32[]{:S(2)}) collective-permute-start(bf16[128,1024]{1,0:T(8,128)(2,1)S(1)} %collective-permute-done.7), channel_id=1, source_target_pairs={{0,1},{1,2},{2,3},{3,0},{4,5},{5,6},{6,7},{7,4},{8,9},{9,10},{10,1... | collective-permute-start | bytes 786440 | tf_op jit(solution)/shard_map/ppermute | solution.py:25
  392.0 53.9 %reduce-scatter.23.cloned.1.call-start = ((), (), s32[]{:S(2)}) async-start(), calls=%async_computation.22 | async-start | bytes 1310720 | tf_op jit(solution)/shard_map/reduce_scatter | solution.py:40
  396.8 118.9 %reduce-scatter.27.cloned.1.call-start = ((), (), s32[]{:S(2)}) async-start(), calls=%async_computation.25 | async-start | bytes 1310720 | tf_op jit(solution)/shard_map/reduce_scatter | solution.py:40
  448.0 8.5 collective-permute-start.10
  456.5 8.6 collective-permute-start.11
  465.1 7.9 collective-permute-start.12
  488.9 91.4 %reduce-scatter.29.cloned.1.call-start = ((), (), s32[]{:S(2)}) async-start(), calls=%async_computation.26 | async-start | bytes 1310720 | tf_op jit(solution)/shard_map/reduce_scatter | solution.py:40
  518.1 8.6 collective-permute-start.13
  526.7 8.6 collective-permute-start.14
  535.3 7.9 collective-permute-start.15
  553.5 116.8 %reduce-scatter.39.cloned.1.call-start = ((), (), s32[]{:S(2)}) async-start(), calls=%async_computation.31 | async-start | bytes 655360 | tf_op jit(solution)/shard_map/reduce_scatter | solution.py:299
  583.9 8.7 collective-permute-start.16
  587.2 83.1 %reduce-scatter.37.cloned.1.call-start = ((), (), s32[]{:S(2)}) async-start(), calls=%async_computation.30 | async-start | bytes 655360 | tf_op jit(solution)/shard_map/reduce_scatter | solution.py:299
  592.6 8.6 collective-permute-start.17
  601.2 8.3 collective-permute-start.18
  614.7 65.3 %reduce-scatter.47.cloned.1.call-start = ((), (), s32[]{:S(2)}) async-start(), calls=%async_computation.35 | async-start | bytes 2621440 | tf_op jit(solution)/shard_map/reduce_scatter | solution.py:299
  619.6 98.5 %reduce-scatter.45.cloned.1.call-start = ((), (), s32[]{:S(2)}) async-start(), calls=%async_computation.34 | async-start | bytes 2621440 | tf_op jit(solution)/shard_map/reduce_scatter | solution.py:299
  624.5 131.8 %reduce-scatter.43.cloned.1.call-start = ((), (), s32[]{:S(2)}) async-start(), calls=%async_computation.33 | async-start | bytes 2621440 | tf_op jit(solution)/shard_map/reduce_scatter | solution.py:299
  628.8 165.7 %reduce-scatter.41.cloned.1.call-start = ((), (), s32[]{:S(2)}) async-start(), calls=%async_computation.32 | async-start | bytes 2621440 | tf_op jit(solution)/shard_map/reduce_scatter | solution.py:299
  633.1 189.6 %reduce-scatter.31.cloned.1.call-start = ((), (), s32[]{:S(2)}) async-start(), calls=%async_computation.27 | async-start | bytes 1310720 | tf_op jit(solution)/shard_map/reduce_scatter | solution.py:40
  645.0 212.2 %reduce-scatter.35.cloned.1.call-start = ((), (), s32[]{:S(2)}) async-start(), calls=%async_computation.29 | async-start | bytes 1966080 | tf_op jit(solution)/shard_map/reduce_scatter | solution.py:299
  649.5 13.5 %all-to-all-start = ((bf16[128,4,256]{2,0,1:T(8,128)(2,1)}), bf16[128,4,256]{2,0,1:T(8,128)(2,1)S(1)}, u32[]{:S(2)}, u32[]{:S(2)}) async-start(bf16[128,4,256]{2,0,1:T(8,128)(2,1)} %bitcast.222), calls=%async_computation.4 | async-start | bytes 524288 | tf_op jit(solution)/shard_map/all_to_all | solution.py:310
  656.7 234.6 %reduce-scatter.33.cloned.1.call-start = ((), (), s32[]{:S(2)}) async-start(), calls=%async_computation.28 | async-start | bytes 1966080 | tf_op jit(solution)/shard_map/reduce_scatter | solution.py:299
  663.1 1.6 collective-permute-start.9
  671.3 1.4 collective-permute-start.21
  671.7 152.2 %copy-start.13 = (f32[128,1024]{1,0:T(8,128)S(1)}, f32[128,1024]{1,0:T(8,128)}, u32[]{:S(2)}) copy-start(f32[128,1024]{1,0:T(8,128)} %get-tuple-element.48) | copy-start | bytes 1572868
  720.0 111.8 %copy-start.16 = (bf16[1024,256]{1,0:T(8,128)(2,1)S(1)}, bf16[1024,256]{1,0:T(8,128)(2,1)}, u32[]{:S(2)}) copy-start(bf16[1024,256]{1,0:T(8,128)(2,1)} %reduce-scatter.47.cloned.1.call-done) | copy-start | bytes 1572868
  720.0 111.8 %copy-start.17 = (bf16[1024,256]{1,0:T(8,128)(2,1)S(1)}, bf16[1024,256]{1,0:T(8,128)(2,1)}, u32[]{:S(2)}) copy-start(bf16[1024,256]{1,0:T(8,128)(2,1)} %reduce-scatter.45.cloned.1.call-done) | copy-start | bytes 1572868
  720.0 111.8 %collective-permute-start.23 = (bf16[1024,256]{1,0:T(8,128)(2,1)}, bf16[1024,256]{1,0:T(8,128)(2,1)}, u32[]{:S(2)}, u32[]{:S(2)}) collective-permute-start(bf16[1024,256]{1,0:T(8,128)(2,1)} %broadcast_select_fusion), channel_id=1, source_target_pairs={{0,16},{16,0},{1,17},{17,1},{2,18},{18,2},{3,19},{19,3},{4,20},{20... | collective-permute-start | bytes 1572872 | tf_op jit(solution)/shard_map/ppermute | solution.py:196
  795.6 97.5 %collective-permute-start.22 = (bf16[256,1024]{1,0:T(8,128)(2,1)S(1)}, bf16[256,1024]{1,0:T(8,128)(2,1)}, u32[]{:S(2)}, u32[]{:S(2)}) collective-permute-start(bf16[256,1024]{1,0:T(8,128)(2,1)S(1)} %broadcast_select_fusion.1), channel_id=1, source_target_pairs={{0,16},{16,0},{1,17},{17,1},{2,18},{18,2},{3,19},{19,3},{4,20},{20... | collective-permute-start | bytes 1572872 | tf_op jit(solution)/shard_map/ppermute | solution.py:196
  825.8 12.9 %all-to-all-start.1 = ((bf16[128,4,256]{2,0,1:T(8,128)(2,1)}), bf16[128,4,256]{2,0,1:T(8,128)(2,1)S(1)}, u32[]{:S(2)}, u32[]{:S(2)}) async-start(bf16[128,4,256]{2,0,1:T(8,128)(2,1)} %bitcast.221), calls=%async_computation.9 | async-start | bytes 524288 | tf_op jit(solution)/shard_map/all_to_all | solution.py:310
  831.8 189.5 %all-reduce.3.cloned.1.call-start = ((), (), s32[]{:S(2)}) async-start(), calls=%async_computation.43 | async-start | bytes 196608
  834.0 59.1 %copy-start.14 = (bf16[256,1024]{1,0:T(8,128)(2,1)S(1)}, bf16[256,1024]{1,0:T(8,128)(2,1)}, u32[]{:S(2)}) copy-start(bf16[256,1024]{1,0:T(8,128)(2,1)} %reduce-scatter.43.cloned.1.call-done) | copy-start | bytes 1572868
  834.0 59.1 %copy-start.15 = (bf16[256,1024]{1,0:T(8,128)(2,1)S(1)}, bf16[256,1024]{1,0:T(8,128)(2,1)}, u32[]{:S(2)}) copy-start(bf16[256,1024]{1,0:T(8,128)(2,1)} %reduce-scatter.41.cloned.1.call-done) | copy-start | bytes 1572868
  840.5 186.9 %collective-permute-start.19 = (bf16[512,256]{1,0:T(8,128)(2,1)}, bf16[512,256]{1,0:T(8,128)(2,1)}, u32[]{:S(2)}, u32[]{:S(2)}) collective-permute-start(bf16[512,256]{1,0:T(8,128)(2,1)} %get-tuple-element.55), channel_id=1, source_target_pairs={{0,16},{16,0},{1,17},{17,1},{2,18},{18,2},{3,19},{19,3},{4,20},{20... | collective-permute-start | bytes 786440 | tf_op jit(solution)/shard_map/ppermute | solution.py:196
  893.1 136.3 %copy-start.19 = (bf16[256,4,192]{0,2,1:T(8,128)(2,1)S(1)}, bf16[256,4,192]{0,2,1:T(8,128)(2,1)}, u32[]{:S(2)}) copy-start(bf16[256,4,192]{0,2,1:T(8,128)(2,1)} %reduce-scatter.35.cloned.1.call-done) | copy-start | bytes 1179652
  893.1 136.3 %copy-start.20 = (bf16[256,4,192]{0,2,1:T(8,128)(2,1)S(1)}, bf16[256,4,192]{0,2,1:T(8,128)(2,1)}, u32[]{:S(2)}) copy-start(bf16[256,4,192]{0,2,1:T(8,128)(2,1)} %reduce-scatter.33.cloned.1.call-done) | copy-start | bytes 1179652
  893.1 136.3 %collective-permute-start.20 = (bf16[256,4,192]{0,2,1:T(8,128)(2,1)}, bf16[256,4,192]{0,2,1:T(8,128)(2,1)S(1)}, u32[]{:S(2)}, u32[]{:S(2)}) collective-permute-start(bf16[256,4,192]{0,2,1:T(8,128)(2,1)} %broadcast_select_fusion.2), channel_id=1, source_target_pairs={{0,16},{16,0},{1,17},{17,1},{2,18},{18,2},{3,19},{19,3},{4,20},{20... | collective-permute-start | bytes 1179656 | tf_op jit(solution)/shard_map/ppermute | solution.py:196
  893.2 137.3 %copy-start.1 = (bf16[1024,256]{1,0:T(8,128)(2,1)S(1)}, bf16[1024,256]{1,0:T(8,128)(2,1)}, u32[]{:S(2)}) copy-start(bf16[1024,256]{1,0:T(8,128)(2,1)} %param.15) | copy-start | bytes 1572868
  (52 other events, 582.2 us)
Sparse Core Ops, SparseCore 0:
  9.8 31.8 all-gather.22
  43.9 31.2 all-gather.18
  76.7 9.6 all-gather.24
  87.7 10.1 all-gather.26
  99.7 36.1 all-gather.28
  137.6 35.0 all-gather.32
  175.5 25.2 reduce-scatter.16
  202.3 14.5 all-gather.30
  218.4 14.8 all-gather.34
  238.7 26.3 reduce-scatter.18
  308.0 26.6 reduce-scatter.20
  336.7 38.4 all-gather.20
  392.1 25.7 reduce-scatter.24
  420.0 25.7 reduce-scatter.22
  489.0 26.6 reduce-scatter.26
  553.6 26.6 reduce-scatter.28
  587.4 26.5 reduce-scatter.38
  616.6 25.0 reduce-scatter.36
  644.7 35.3 reduce-scatter.46
  682.9 35.2 reduce-scatter.44
  721.1 35.1 reduce-scatter.42
  759.3 35.1 reduce-scatter.40
  797.4 25.2 reduce-scatter.30
  825.5 31.6 reduce-scatter.34
  860.2 31.1 reduce-scatter.32
  896.8 124.5 all-reduce.2
